TPU v7x, 32 devices: a whole 2x2x4 slice. The times are simulated.
32 devices in a mesh: stn: 2 (over x), vox: 16 (over z, y, core).
Axes of the slice: x: 2, y: 2, z: 4, core: 2. Of those that a mesh axis runs over, the one named last changes fastest.
Arguments:
- voltages: bfloat16 [56, 2, 65536], P('stn', None, 'vox'), may hold values from -6 to 6
- sample_delays: int32 [56, 65536], P(None, 'vox'), may hold values from 0 to 239
- timing_offsets: int32 [56], replicated, may hold values from 0 to 15
- reference_station: int32 [1], replicated, may hold values from 0 to 55
Outputs:
- image_out: float32 [64, 65536], P('stn', 'vox')
All inputs are finite; a program needn't handle non-finite values.
Results may differ from a plain program's by a relative error of at most 0.004.
Values may be sent and summed in bfloat16 or wider, within the bound.
No kernel may reach another device: no remote copies, remote signals or barrier semaphores. Data moves between devices by JAX's collectives and lax.ppermute only.
A program may use at most 64 MiB of HBM per device.

v0:
```python
import math
import jax
import jax.numpy as jnp
from jax import lax
from jax.sharding import PartitionSpec as P

STATIONS = 56
WIN = 1024
LAGS = 256


def spread(value, axis, source):
    kept = jnp.where(lax.axis_index(axis) == source, value, 0).astype(value.dtype)
    return lax.psum(kept, axis)


def padded(block, sides, width):
    for axis, dim in sides:
        count = lax.axis_size(axis)
        forward = [(i, i + 1) for i in range(count - 1)]
        backward = [(target, source) for source, target in forward]
        low = lax.ppermute(
            lax.slice_in_dim(block, block.shape[dim] - width, None, axis=dim), axis, forward
        )
        high = lax.ppermute(lax.slice_in_dim(block, 0, width, axis=dim), axis, backward)
        block = jnp.concatenate([low, block, high], axis=dim)
    return block


def taper_weights(length):
    position = (jnp.arange(length, dtype=jnp.float32) + 0.5) / length
    return 0.5 - 0.5 * jnp.cos(2.0 * math.pi * position)


def shards(voltages, sample_delays, timing_offsets, reference_station):
    stations_here, polarizations, samples_here = voltages.shape
    slices_here = samples_here // WIN
    voxels_here = sample_delays.shape[1]
    station_ref = reference_station[0]
    stn_index = lax.axis_index("stn")
    taper_curve = taper_weights(WIN)
    norm_inv = 1.0 / jnp.sqrt(jnp.sum(taper_curve * taper_curve))
    owner_index = station_ref // stations_here
    ref_local = lax.dynamic_index_in_dim(voltages, station_ref % stations_here, 0, keepdims=False)
    ref_signal = spread(ref_local, "stn", owner_index)
    extended = padded(ref_signal, (("vox", 1),), LAGS // 2)
    extended = jnp.pad(extended, ((0, 0), (0, WIN)))
    leading = extended[:, :samples_here].reshape(polarizations, slices_here, WIN)
    trailing = extended[:, WIN : samples_here + WIN].reshape(polarizations, slices_here, WIN)[
        :, :, : LAGS - 1
    ]
    segments = jnp.concatenate([leading, trailing], axis=2).reshape(
        1, polarizations * slices_here, WIN + LAGS - 1
    )
    windowed = (
        voltages.reshape(stations_here, polarizations, slices_here, WIN) * taper_curve
    ).astype(jnp.bfloat16)
    kernels = jnp.transpose(windowed, (1, 2, 0, 3)).reshape(
        polarizations * slices_here * stations_here, 1, WIN
    )
    lagged_sums = lax.conv_general_dilated(
        segments,
        kernels,
        (1,),
        "VALID",
        feature_group_count=polarizations * slices_here,
        preferred_element_type=jnp.float32,
    )
    lagged_sums = jnp.sum(
        lagged_sums.reshape(polarizations, slices_here, stations_here, LAGS), axis=0
    )
    station_ids = stn_index * stations_here + jnp.arange(stations_here, dtype=jnp.int32)
    keep_mask = (station_ids != station_ref).astype(jnp.float32)
    local_corr = (
        jnp.transpose(lagged_sums, (1, 0, 2)) * keep_mask[:, None, None] * norm_inv
    ).astype(jnp.bfloat16)
    corr_all = lax.all_gather(local_corr, "vox", axis=1, tiled=True)
    lag_index = sample_delays + timing_offsets[:, None]
    total_slices = corr_all.shape[1]
    out_scale = 1.0 / math.sqrt(2.0 * STATIONS)
    my_lags = lax.dynamic_slice_in_dim(lag_index, stn_index * stations_here, stations_here, 0)
    corr_block = lax.slice_in_dim(
        corr_all, 0, lax.axis_size("stn") * (total_slices // lax.axis_size("stn")), axis=1
    )
    lag_grid = lax.broadcasted_iota(jnp.int32, (LAGS, voxels_here), 0)

    def add_station(running, inputs_pair):
        corr_rows, lags_one = inputs_pair
        selector = (lag_grid == lags_one[None, :]).astype(jnp.bfloat16)
        return (running + jnp.dot(corr_rows, selector, preferred_element_type=jnp.float32), None)

    running, unused = lax.scan(
        add_station,
        jnp.zeros(
            (lax.axis_size("stn") * (total_slices // lax.axis_size("stn")), voxels_here),
            jnp.float32,
        ),
        (corr_block, my_lags),
    )
    image_out = lax.psum_scatter(running, "stn", scatter_dimension=0, tiled=True)
    return image_out * out_scale


def solution(mesh):
    return jax.shard_map(
        shards,
        mesh=mesh,
        in_specs=(P("stn", None, "vox"), P(None, "vox"), P(), P()),
        out_specs=P("stn", "vox"),
        check_vma=False,
    )
```

profile of v0, /device:TPU:0, one launch (start us, length us, event | category | flops | bytes accessed | tf_op | source)
XLA Modules:
  0.0 126.3 jit_solution(5938789996437528588)
XLA Ops:
  8.0 9.7 %psum.7 = bf16[2,4096]{1,0:T(2,128)(2,1)S(1)} all-reduce(bf16[2,4096]{1,0:T(2,128)(2,1)S(1)} %fusion.14), channel_id=1, replica_groups=mesh['stn'=2,'vox'=16] {'stn'}, use_global_device_ids=true, to_apply=%region_0.0 | all-reduce | flops 8192 | bytes 32768 | tf_op jit(solution)/shard_map/psum | solution.py:14
  17.6 1.3 %collective-permute-start = (bf16[2,128]{1,0:T(2,128)(2,1)S(1)}, bf16[2,128]{1,0:T(2,128)(2,1)S(1)}, u32[]{:S(2)}, u32[]{:S(2)}) collective-permute-start(bf16[2,128]{1,0:T(2,128)(2,1)S(1)} %get-tuple-element.64), channel_id=1, source_target_pairs={{0,1},{1,2},{2,3},{3,4},{4,5},{5,6},{6,7},{7,8},{8,9},{9,10},{10,1... | collective-permute-start | bytes 1544 | tf_op jit(solution)/shard_map/ppermute | solution.py:22
  18.9 1.3 %collective-permute-start.1 = (bf16[2,128]{1,0:T(2,128)(2,1)S(1)}, bf16[2,128]{1,0:T(2,128)(2,1)S(1)}, u32[]{:S(2)}, u32[]{:S(2)}) collective-permute-start(bf16[2,128]{1,0:T(2,128)(2,1)S(1)} %get-tuple-element.65), channel_id=1, source_target_pairs={{1,0},{2,1},{3,2},{4,3},{5,4},{6,5},{7,6},{8,7},{9,8},{10,9},{11,1... | collective-permute-start | bytes 1544 | tf_op jit(solution)/shard_map/ppermute | solution.py:25
  20.2 1.4 %reshape.40 = f32[28,2,4,1024]{3,2,1,0:T(4,128)S(1)} reshape(bf16[28,2,4096]{2,1,0:T(2,128)(2,1)} %param.6) | data formatting | bytes 1376256 | tf_op jit(solution)/shard_map/convert_element_type | solution.py:56
  25.6 16.9 %fusion.7 = f32[1,224,256]{1,0,2:T(1,128)S(1)} fusion(bf16[1,8,1279]{1,0,2:T(2,128)(2,1)S(1)} %copy.13, s32[224]{0:T(256)S(1)} %copy-done.3, bf16[224,1024]{0,1:T(8,128)(2,1)S(1)} %copy.12), kind=kOutput, calls=%fused_computation.10 | convolution fusion | flops 943194112 | bytes 709488 | tf_op jit(solution)/shard_map/conv_general_dilated | solution.py:61
  42.8 27.5 %all_gather.3 = bf16[28,64,256]{2,0,1:T(8,128)(2,1)S(1)} all-gather(bf16[28,4,256]{2,0,1:T(8,128)(2,1)S(1)} %fusion.13), channel_id=1, replica_groups=mesh['stn'=2,'vox'=16] {'vox'}, dimensions={1}, use_global_device_ids=true | all-gather | bytes 974848 | tf_op jit(solution)/shard_map/all_gather | solution.py:77
  70.9 28.9 %while.11 = (s32[]{:T(128)}, f32[64,4096]{1,0:T(8,128)S(1)}, bf16[28,64,256]{2,1,0:T(8,128)(2,1)S(1)}, s32[28,4096]{1,0:T(8,128)S(1)}, s32[]{:T(128)}, /*index=5*/s32[]{:T(128)}) while((s32[]{:T(128)}, f32[64,4096]{1,0:T(8,128)S(1)}, bf16[28,64,256]{2,1,0:T(8,128)(2,1)S(1)}, s32[28,4096]{1,0:T(8,128)S(1)}, s32[]{:T(128)}, ...), condition=%wide.region_4.5_spmd.clone, body=%wide.region_3.4_spmd.clone.sunk | while | flops 135790592 | bytes 2179159 | solution.py:92
  70.9 1.0 convolution_add_fusion.2
  72.0 1.0 convolution_add_fusion.2
  73.0 1.0 convolution_add_fusion.2
  74.0 1.0 convolution_add_fusion.2
  75.1 1.0 convolution_add_fusion.2
  76.1 1.0 convolution_add_fusion.2
  77.1 1.0 convolution_add_fusion.2
  78.1 1.0 convolution_add_fusion.2
  79.2 1.0 convolution_add_fusion.2
  80.2 1.0 convolution_add_fusion.2
  81.2 1.0 convolution_add_fusion.2
  82.3 1.0 convolution_add_fusion.2
  83.3 1.0 convolution_add_fusion.2
  84.3 1.0 convolution_add_fusion.2
  85.4 1.0 convolution_add_fusion.2
  87.4 1.0 convolution_add_fusion.2
  89.5 1.0 convolution_add_fusion.2
  90.5 1.0 convolution_add_fusion.2
  91.6 1.0 convolution_add_fusion.2
  93.6 1.0 convolution_add_fusion.2
  95.7 1.0 convolution_add_fusion.2
  97.7 1.0 convolution_add_fusion.2
  99.8 1.0 copy-done
  100.8 16.8 %reduce-scatter.2.cloned.1.call-done = f32[32,4096]{1,0:T(8,128)} async-done(((f32[64,4096]{1,0:T(8,128)}), f32[32,4096]{1,0:T(8,128)}) %reduce-scatter.2.cloned.1.call-update) | async-done | bytes 524304 | tf_op jit(solution)/shard_map/reduce_scatter | solution.py:100
  117.6 1.9 %broadcast_multiply_fusion = f32[32,4096]{1,0:T(8,128)} fusion(f32[32,4096]{1,0:T(8,128)} %reduce-scatter.2.cloned.1.call-done), kind=kLoop, calls=%fused_computation.17 | loop fusion | flops 131072 | bytes 1048576 | tf_op jit(solution)/shard_map/mul | solution.py:101
  (68 shorter events, 11.2 us)
Async XLA Ops:
  6.5 111.1 %reduce-scatter.2.cloned.1.call-start = ((), (), s32[]{:S(2)}) async-start(), calls=%async_computation.1 | async-start | bytes 1572864 | tf_op jit(solution)/shard_map/reduce_scatter | solution.py:100
  17.6 6.9 %collective-permute-start = (bf16[2,128]{1,0:T(2,128)(2,1)S(1)}, bf16[2,128]{1,0:T(2,128)(2,1)S(1)}, u32[]{:S(2)}, u32[]{:S(2)}) collective-permute-start(bf16[2,128]{1,0:T(2,128)(2,1)S(1)} %get-tuple-element.64), channel_id=1, source_target_pairs={{0,1},{1,2},{2,3},{3,4},{4,5},{5,6},{6,7},{7,8},{8,9},{9,10},{10,1... | collective-permute-start | bytes 1544 | tf_op jit(solution)/shard_map/ppermute | solution.py:22
  18.9 5.6 %collective-permute-start.1 = (bf16[2,128]{1,0:T(2,128)(2,1)S(1)}, bf16[2,128]{1,0:T(2,128)(2,1)S(1)}, u32[]{:S(2)}, u32[]{:S(2)}) collective-permute-start(bf16[2,128]{1,0:T(2,128)(2,1)S(1)} %get-tuple-element.65), channel_id=1, source_target_pairs={{1,0},{2,1},{3,2},{4,3},{5,4},{6,5},{7,6},{8,7},{9,8},{10,9},{11,1... | collective-permute-start | bytes 1544 | tf_op jit(solution)/shard_map/ppermute | solution.py:25
  21.7 0.7 copy-start.2
  21.7 1.2 copy-start.1
  23.1 2.5 %copy-start.3 = (s32[224]{0:T(256)S(1)}, s32[224]{0:T(256)}, u32[]{:S(2)}) copy-start(s32[224]{0:T(256)} %constant.54.clone.1) | copy-start | bytes 2692
  99.8 1.0 copy-start
Sparse Core Ops, SparseCore 0:
  100.9 16.6 reduce-scatter.1
where the time goes:
time: 127 us; the launch traced here: 126 us
  matrix products  44.3 us (35%)
  blocking collectives  37.2 us (29%)
  waiting for transfers between devices  16.8 us (13%)
  between operations  14.9 us (12%)
  local copies, waits for them, and re-layouts  5.49 us (4%)
  other arithmetic  4.06 us (3%)
  starting transfers between devices  2.58 us (2%)
    all_gather x1, blocking collectives, shards(): corr_all = lax.all_gather(local_corr, 'vox', axis=1, tiled=True)  27.5 us
    dot_general x28, matrix products, add_station(): jnp.dot(corr_rows, selector, preferred_element_type=jnp.float32)  27.4 us
    conv_general_dilated x1, matrix products, shards(): lax.conv_general_dilated(segments, kernels, (1,), 'VALID', feature_group_...  16.9 us
    reduce_scatter x1, waiting for transfers between devices, shards(): lax.psum_scatter(running, 'stn', scatter_dimension=0, tiled=True)  16.8 us
    psum x1, blocking collectives, spread(): return lax.psum(kept, axis)  9.65 us
  transfers between devices with their start and end apart: 3, of which 1 were waited for; matrix products, arithmetic and copies ran while one was open for 2% of the time, Pallas kernels for 0%

commit v1 on v0

--- a/solution.py
+++ b/solution.py
@@ -9,9 +9,15 @@
 LAGS = 256
 
 
+def add_all(block, name):
+    shards = lax.all_gather(block, name, axis=0, tiled=False)
+    total = shards.sum(axis=0)
+    return total
+
+
 def spread(value, axis, source):
     kept = jnp.where(lax.axis_index(axis) == source, value, 0).astype(value.dtype)
-    return lax.psum(kept, axis)
+    return add_all(kept, axis)
 
 
 def padded(block, sides, width):

time: 127 us -> 124 us (0.976)
  blocking collectives: 37.2 us -> 33.5 us
    psum x1 -> x0, blocking collectives: 9.65 us -> none  [spread(): return lax.psum(kept, axis)]
    all_gather x0 -> x1, blocking collectives: none -> 5.31 us  [add_all(): shards = lax.all_gather(block, name, axis=0, tiled=False)]
  transfers between devices with their start and end apart: 3 -> 3, of which waited for: 1 -> 1; matrix products, arithmetic and copies ran while one was open for 2% -> 3% of each run, Pallas kernels for 0% -> 0%
where the time goes in v1:
time: 124 us; the launch traced here: 123 us
  matrix products  44.2 us (36%)
  blocking collectives  33.5 us (27%)
  waiting for transfers between devices  17.8 us (14%)
  between operations  14.9 us (12%)
  local copies, waits for them, and re-layouts  5.31 us (4%)
  other arithmetic  4.1 us (3%)
  starting transfers between devices  2.58 us (2%)
    all_gather x1, blocking collectives, shards(): corr_all = lax.all_gather(local_corr, 'vox', axis=1, tiled=True)  28.2 us
    dot_general x28, matrix products, add_station(): jnp.dot(corr_rows, selector, preferred_element_type=jnp.float32)  27.4 us
    reduce_scatter x1, waiting for transfers between devices, shards(): lax.psum_scatter(running, 'stn', scatter_dimension=0, tiled=True)  17.8 us
    conv_general_dilated x1, matrix products, shards(): lax.conv_general_dilated(segments, kernels, (1,), 'VALID', feature_group_...  16.9 us
    all_gather x1, blocking collectives, add_all(): shards = lax.all_gather(block, name, axis=0, tiled=False)  5.31 us
  transfers between devices with their start and end apart: 3, of which 1 were waited for; matrix products, arithmetic and copies ran while one was open for 3% of the time, Pallas kernels for 0%

profile of v1, /device:TPU:0, one launch (start us, length us, event | category | flops | bytes accessed | tf_op | source)
XLA Modules:
  0.0 123.4 jit_solution(9715656799755949595)
XLA Ops:
  8.0 5.3 %all_gather.7 = bf16[2,2,4096]{2,1,0:T(2,128)(2,1)S(1)} all-gather(bf16[1,2,4096]{2,1,0:T(2,128)(2,1)S(1)} %broadcast_select_fusion), channel_id=1, replica_groups=mesh['stn'=2,'vox'=16] {'stn'}, dimensions={0}, use_global_device_ids=true | all-gather | bytes 49152 | tf_op jit(solution)/shard_map/all_gather | solution.py:13
  13.3 1.3 %collective-permute-start = (bf16[2,128]{1,0:T(2,128)(2,1)S(1)}, bf16[2,128]{1,0:T(2,128)(2,1)S(1)}, u32[]{:S(2)}, u32[]{:S(2)}) collective-permute-start(bf16[2,128]{1,0:T(2,128)(2,1)S(1)} %get-tuple-element.64), channel_id=1, source_target_pairs={{0,1},{1,2},{2,3},{3,4},{4,5},{5,6},{6,7},{7,8},{8,9},{9,10},{10,1... | collective-permute-start | bytes 1544 | tf_op jit(solution)/shard_map/ppermute | solution.py:28
  14.6 1.3 %collective-permute-start.1 = (bf16[2,128]{1,0:T(2,128)(2,1)S(1)}, bf16[2,128]{1,0:T(2,128)(2,1)S(1)}, u32[]{:S(2)}, u32[]{:S(2)}) collective-permute-start(bf16[2,128]{1,0:T(2,128)(2,1)S(1)} %get-tuple-element.65), channel_id=1, source_target_pairs={{1,0},{2,1},{3,2},{4,3},{5,4},{6,5},{7,6},{8,7},{9,8},{10,9},{11,1... | collective-permute-start | bytes 1544 | tf_op jit(solution)/shard_map/ppermute | solution.py:31
  15.9 1.4 %reshape.37 = f32[28,2,4,1024]{3,2,1,0:T(4,128)S(1)} reshape(bf16[28,2,4096]{2,1,0:T(2,128)(2,1)} %param.6) | data formatting | bytes 1376256 | tf_op jit(solution)/shard_map/convert_element_type | solution.py:62
  21.1 16.9 %fusion.7 = f32[1,224,256]{1,0,2:T(1,128)S(1)} fusion(bf16[1,8,1279]{1,0,2:T(2,128)(2,1)S(1)} %copy.12, s32[224]{0:T(256)S(1)} %copy-done.3, bf16[224,1024]{0,1:T(8,128)(2,1)S(1)} %copy.11), kind=kOutput, calls=%fused_computation.10 | convolution fusion | flops 943194112 | bytes 709488 | tf_op jit(solution)/shard_map/conv_general_dilated | solution.py:67
  38.3 28.2 %all_gather.8 = bf16[28,64,256]{2,0,1:T(8,128)(2,1)S(1)} all-gather(bf16[28,4,256]{2,0,1:T(8,128)(2,1)S(1)} %fusion.13), channel_id=1, replica_groups=mesh['stn'=2,'vox'=16] {'vox'}, dimensions={1}, use_global_device_ids=true | all-gather | bytes 974848 | tf_op jit(solution)/shard_map/all_gather | solution.py:83
  67.0 28.9 %while.11 = (s32[]{:T(128)}, f32[64,4096]{1,0:T(8,128)S(1)}, bf16[28,64,256]{2,1,0:T(8,128)(2,1)S(1)}, s32[28,4096]{1,0:T(8,128)S(1)}, s32[]{:T(128)}, /*index=5*/s32[]{:T(128)}) while((s32[]{:T(128)}, f32[64,4096]{1,0:T(8,128)S(1)}, bf16[28,64,256]{2,1,0:T(8,128)(2,1)S(1)}, s32[28,4096]{1,0:T(8,128)S(1)}, s32[]{:T(128)}, ...), condition=%wide.region_4.5_spmd.clone, body=%wide.region_3.4_spmd.clone.sunk | while | flops 135790592 | bytes 2179159 | solution.py:98
  67.0 1.0 convolution_add_fusion.2
  68.0 1.0 convolution_add_fusion.2
  69.1 1.0 convolution_add_fusion.2
  70.1 1.0 convolution_add_fusion.2
  71.1 1.0 convolution_add_fusion.2
  72.2 1.0 convolution_add_fusion.2
  73.2 1.0 convolution_add_fusion.2
  74.2 1.0 convolution_add_fusion.2
  75.3 1.0 convolution_add_fusion.2
  76.3 1.0 convolution_add_fusion.2
  77.3 1.0 convolution_add_fusion.2
  78.4 1.0 convolution_add_fusion.2
  79.4 1.0 convolution_add_fusion.2
  80.4 1.0 convolution_add_fusion.2
  81.5 1.0 convolution_add_fusion.2
  83.5 1.0 convolution_add_fusion.2
  85.6 1.0 convolution_add_fusion.2
  86.6 1.0 convolution_add_fusion.2
  87.6 1.0 convolution_add_fusion.2
  89.7 1.0 convolution_add_fusion.2
  91.8 1.0 convolution_add_fusion.2
  93.8 1.0 convolution_add_fusion.2
  95.9 1.0 copy-done
  96.9 17.8 %reduce-scatter.2.cloned.1.call-done = f32[32,4096]{1,0:T(8,128)} async-done(((f32[64,4096]{1,0:T(8,128)}), f32[32,4096]{1,0:T(8,128)}) %reduce-scatter.2.cloned.1.call-update) | async-done | bytes 524304 | tf_op jit(solution)/shard_map/reduce_scatter | solution.py:106
  114.6 1.9 %broadcast_multiply_fusion = f32[32,4096]{1,0:T(8,128)} fusion(f32[32,4096]{1,0:T(8,128)} %reduce-scatter.2.cloned.1.call-done), kind=kLoop, calls=%fused_computation.17 | loop fusion | flops 131072 | bytes 1048576 | tf_op jit(solution)/shard_map/mul | solution.py:107
  (69 shorter events, 11.0 us)
Async XLA Ops:
  6.5 108.1 %reduce-scatter.2.cloned.1.call-start = ((), (), s32[]{:S(2)}) async-start(), calls=%async_computation.1 | async-start | bytes 1572864 | tf_op jit(solution)/shard_map/reduce_scatter | solution.py:106
  13.3 6.9 %collective-permute-start = (bf16[2,128]{1,0:T(2,128)(2,1)S(1)}, bf16[2,128]{1,0:T(2,128)(2,1)S(1)}, u32[]{:S(2)}, u32[]{:S(2)}) collective-permute-start(bf16[2,128]{1,0:T(2,128)(2,1)S(1)} %get-tuple-element.64), channel_id=1, source_target_pairs={{0,1},{1,2},{2,3},{3,4},{4,5},{5,6},{6,7},{7,8},{8,9},{9,10},{10,1... | collective-permute-start | bytes 1544 | tf_op jit(solution)/shard_map/ppermute | solution.py:28
  14.6 5.6 %collective-permute-start.1 = (bf16[2,128]{1,0:T(2,128)(2,1)S(1)}, bf16[2,128]{1,0:T(2,128)(2,1)S(1)}, u32[]{:S(2)}, u32[]{:S(2)}) collective-permute-start(bf16[2,128]{1,0:T(2,128)(2,1)S(1)} %get-tuple-element.65), channel_id=1, source_target_pairs={{1,0},{2,1},{3,2},{4,3},{5,4},{6,5},{7,6},{8,7},{9,8},{10,9},{11,1... | collective-permute-start | bytes 1544 | tf_op jit(solution)/shard_map/ppermute | solution.py:31
  17.4 0.7 copy-start.2
  17.4 1.2 copy-start.1
  18.8 2.3 %copy-start.3 = (s32[224]{0:T(256)S(1)}, s32[224]{0:T(256)}, u32[]{:S(2)}) copy-start(s32[224]{0:T(256)} %constant.55.clone.1) | copy-start | bytes 2692
  95.9 1.0 copy-start
Sparse Core Ops, SparseCore 0:
  97.0 17.5 reduce-scatter.1
